TPU v7x, 768 devices: a whole 4x8x12 slice. The times are simulated.
768 devices in a mesh: leaf: 96 (over z, y), sub: 8 (over x, core).
Axes of the slice: x: 4, y: 8, z: 12, core: 2. Of those that a mesh axis runs over, the one named last changes fastest.
Arguments:
- start_vec: float32 [3072, 256], P(('leaf', 'sub')), as said below
- near_blocks: bfloat16 [3072, 2, 256, 256], P(('leaf', 'sub')), may hold values from -0.25 to 0.25
- near_ids: int32 [3072, 1], P(('leaf', 'sub')), may hold values from 0 to 95
- far_ids: int32 [3072, 2], P(('leaf', 'sub')), may hold values from 0 to 31
- leaf_basis: bfloat16 [3072, 64, 256], P(('leaf', 'sub')), may hold values from -0.375 to 0.375
- leaf_coupling: bfloat16 [3072, 64, 128], P(('leaf', 'sub')), may hold values from -0.5 to 0.5
- node_transfer: bfloat16 [768, 64, 256], P(('leaf', 'sub')), may hold values from -0.375 to 0.375
- branch_transfer: bfloat16 [768, 64, 64], P(('leaf', 'sub')), may hold values from -0.75 to 0.75
- top_ids: int32 [96, 4], P('leaf'), may hold values from 0 to 95
- top_coupling: bfloat16 [96, 64, 256], P('leaf'), may hold values from -0.375 to 0.375
Outputs:
- basis: float32 [4, 3072, 256], P(None, ('leaf', 'sub'))
- hessen: float32 [4, 3], replicated
Inputs may be any that keep to these rules, and one draw needn't show every extreme that they name: start_vec is real-valued with entries of order one.
All inputs are finite; a program needn't handle non-finite values.
Results may differ from a plain program's by a relative error of at most 0.02.
Values may be sent and summed in bfloat16 or wider, within the bound.
A program may use at most 32 MiB of HBM per device.

v0:
```python
import jax
import jax.numpy as jnp
from jax import lax
from jax.sharding import PartitionSpec as P

MATVECS = 3


def with_halo(cells, sides, width):
    for axis, dim in sides:
        count = lax.axis_size(axis)
        ends = count - 1
        head = lax.slice_in_dim(cells, 0, width, axis=dim)
        tail = lax.slice_in_dim(cells, cells.shape[dim] - width, cells.shape[dim], axis=dim)
        cells = jnp.concatenate(
            [
                lax.ppermute(tail, axis, [(i, (i + 1) % count) for i in range(ends)]),
                cells,
                lax.ppermute(head, axis, [((i + 1) % count, i) for i in range(ends)]),
            ],
            axis=dim,
        )
    return cells


def apply_matrix(
    vector,
    near_blocks,
    near_ids,
    far_ids,
    leaf_basis,
    leaf_coupling,
    node_transfer,
    branch_transfer,
    top_ids,
    top_coupling,
):
    highest = lax.Precision.HIGHEST
    leaves = vector.shape[0]
    branches = lax.axis_size("leaf")
    rank = leaf_basis.shape[1]
    vec_bf = vector.astype(jnp.bfloat16)
    coef_bf = jnp.einsum(
        "lrk,lk->lr", leaf_basis, vec_bf, preferred_element_type=jnp.float32
    ).astype(jnp.bfloat16)
    node_coef = jnp.dot(node_transfer[0], coef_bf.reshape(-1), preferred_element_type=jnp.float32)
    upper_f = branch_transfer[0].astype(jnp.float32)
    node_term = jnp.dot(upper_f, node_coef, precision=highest).astype(jnp.bfloat16)[None, :]
    branch_leafc, branch_terms = (
        lax.all_gather(coef_bf, "sub", axis=0, tiled=True),
        lax.all_gather(node_term, "sub", axis=0, tiled=True),
    )
    own_coef = jnp.sum(branch_terms.astype(jnp.float32), axis=0).astype(jnp.bfloat16)
    branch_table = lax.all_gather(own_coef[None, :], "leaf", axis=0, tiled=True)
    branch_vec = lax.all_gather(vec_bf, "sub", axis=0, tiled=True)
    neighbours = with_halo(branch_vec, (("leaf", 0),), branch_vec.shape[0])
    picked = neighbours[near_ids]
    near_input = jnp.concatenate([vec_bf[:, None, :], picked], axis=1)
    near_out = jnp.einsum(
        "lsij,lsj->li", near_blocks, near_input, preferred_element_type=jnp.float32
    )
    far_coef = branch_leafc[far_ids].reshape(leaves, -1)
    leaf_far = jnp.einsum("lrk,lk->lr", leaf_coupling, far_coef, preferred_element_type=jnp.float32)
    selector = (top_ids[0][:, None] == jnp.arange(branches, dtype=jnp.int32)[None, :]).astype(
        jnp.bfloat16
    )
    partners = jnp.dot(selector, branch_table, preferred_element_type=jnp.float32).astype(
        jnp.bfloat16
    )
    branch_local = jnp.dot(
        top_coupling[0], partners.reshape(-1), preferred_element_type=jnp.float32
    )
    node_local = jnp.dot(branch_local, upper_f, precision=highest)
    leaf_down = jnp.dot(
        node_local, node_transfer[0].astype(jnp.float32), precision=highest
    ).reshape(leaves, rank)
    local_coef = (leaf_down + leaf_far).astype(jnp.bfloat16)
    far_out = jnp.einsum("lrk,lr->lk", leaf_basis, local_coef, preferred_element_type=jnp.float32)
    return 0.5 * vector + near_out + far_out


def per_device(
    start_vec,
    near_blocks,
    near_ids,
    far_ids,
    leaf_basis,
    leaf_coupling,
    node_transfer,
    branch_transfer,
    top_ids,
    top_coupling,
):
    total = float(
        start_vec.shape[0] * start_vec.shape[1] * lax.axis_size("leaf") * lax.axis_size("sub")
    )
    start_sum = lax.psum(jnp.sum(start_vec * start_vec), ("leaf", "sub"))
    first = start_vec * lax.rsqrt(start_sum / total + 1e-06)
    vectors = [first]
    hessen = jnp.zeros((MATVECS + 1, MATVECS), jnp.float32)
    for column in range(MATVECS):
        image = apply_matrix(
            vectors[column],
            near_blocks,
            near_ids,
            far_ids,
            leaf_basis,
            leaf_coupling,
            node_transfer,
            branch_transfer,
            top_ids,
            top_coupling,
        )
        partial_dots = jnp.stack([jnp.sum(earlier * image) for earlier in vectors])
        dot_sums, square_sum = lax.psum((partial_dots, jnp.sum(image * image)), ("leaf", "sub"))
        dots = dot_sums / total
        square = square_sum / total
        remain = square - jnp.sum(dots * dots)
        scale = jnp.sqrt(jnp.maximum(remain, 0.01 * square))
        update = image
        for index_i in range(column + 1):
            update = update - dots[index_i] * vectors[index_i]
        vectors.append(update / scale)
        hessen = hessen.at[: column + 1, column].set(dots)
        hessen = hessen.at[column + 1, column].set(scale)
    return (jnp.stack(vectors), hessen)


def solution(mesh):
    placed = (
        P(("leaf", "sub"), None),
        P(("leaf", "sub"), None, None, None),
        P(("leaf", "sub"), None),
        P(("leaf", "sub"), None),
        P(("leaf", "sub"), None, None),
        P(("leaf", "sub"), None, None),
        P(("leaf", "sub"), None, None),
        P(("leaf", "sub"), None, None),
        P("leaf", None),
        P("leaf", None, None),
    )
    return jax.shard_map(
        per_device,
        mesh=mesh,
        in_specs=placed,
        out_specs=(P(None, ("leaf", "sub"), None), P()),
        check_vma=False,
    )
```

profile of v0, /device:TPU:1, one launch (start us, length us, event | category | flops | bytes accessed | tf_op | source)
XLA Modules:
  0.0 1837.8 jit_solution(1952089322221584401)
XLA Ops:
  2.0 120.4 %psum.49 = f32[]{:T(128)} all-reduce(f32[]{:T(128)} %multiply_reduce_fusion.9), channel_id=1, replica_groups=mesh['leaf'=96,'sub'=8] {'leaf','sub'}, use_global_device_ids=true, to_apply=%region_1.0 | all-reduce | flops 1 | bytes 8 | tf_op jit(solution)/shard_map/psum | solution.py:97
  123.2 11.7 all-gather.6
  136.2 4.0 collective-permute-start
  144.4 12.5 all-reduce.1
  159.3 328.2 %all-reduce.2 = bf16[6144]{0:T(1024)(128)(2,1)S(1)} all-reduce(bf16[6144]{0:T(1024)(128)(2,1)S(1)} %dynamic-update-slice.13), channel_id=3, replica_groups=mesh['leaf'=96,'sub'=8] {'leaf'}, use_global_device_ids=true, to_apply=%add.2 | all-reduce | flops 6144 | bytes 24576
  488.8 90.8 %all-gather.7 = bf16[8,4,64]{2,1,0:T(4,128)(2,1)S(1)} all-gather(bf16[1,4,64]{2,1,0:T(4,128)(2,1)S(1)} %convert_bitcast_fusion.11), channel_id=1, replica_groups=mesh['leaf'=96,'sub'=8] {'sub'}, dimensions={0}, use_global_device_ids=true | all-gather | bytes 4608 | tf_op jit(solution)/shard_map/all_gather | solution.py:50
  585.7 105.1 %all-reduce.9 = (f32[]{:T(128)}, f32[1]{0:T(128)}) all-reduce(f32[]{:T(128)} %get-tuple-element.90, f32[1]{0:T(128)} %bitcast.32), channel_id=1, replica_groups=mesh['leaf'=96,'sub'=8] {'leaf','sub'}, use_global_device_ids=true, to_apply=%region_6.0 | all-reduce | flops 2 | bytes 16 | tf_op jit(solution)/shard_map/psum | solution.py:115
  694.1 11.7 all-gather.8
  707.1 4.0 collective-permute-start.2
  711.7 12.5 all-reduce.3
  724.6 328.6 %all-reduce.4 = bf16[6144]{0:T(1024)(128)(2,1)S(1)} all-reduce(bf16[6144]{0:T(1024)(128)(2,1)S(1)} %dynamic-update-slice.15), channel_id=5, replica_groups=mesh['leaf'=96,'sub'=8] {'leaf'}, use_global_device_ids=true, to_apply=%add.4 | all-reduce | flops 6144 | bytes 24576
  1054.0 90.7 %all-gather.9 = bf16[8,4,64]{2,1,0:T(4,128)(2,1)S(1)} all-gather(bf16[1,4,64]{2,1,0:T(4,128)(2,1)S(1)} %convert_bitcast_fusion.10), channel_id=1, replica_groups=mesh['leaf'=96,'sub'=8] {'sub'}, dimensions={0}, use_global_device_ids=true | all-gather | bytes 4608 | tf_op jit(solution)/shard_map/all_gather | solution.py:50
  1148.8 108.0 %all-reduce.8 = (f32[]{:T(128)}, f32[2]{0:T(128)S(1)}) all-reduce(f32[]{:T(128)} %get-tuple-element.87, f32[2]{0:T(128)S(1)} %pad_maximum_fusion.4), channel_id=1, replica_groups=mesh['leaf'=96,'sub'=8] {'leaf','sub'}, use_global_device_ids=true, to_apply=%region_12.0 | all-reduce | flops 3 | bytes 24 | tf_op jit(solution)/shard_map/psum | solution.py:115
  1261.4 11.7 all-gather.10
  1274.4 4.0 collective-permute-start.4
  1279.0 12.5 all-reduce.5
  1291.9 328.5 %all-reduce.6 = bf16[6144]{0:T(1024)(128)(2,1)S(1)} all-reduce(bf16[6144]{0:T(1024)(128)(2,1)S(1)} %dynamic-update-slice.17), channel_id=7, replica_groups=mesh['leaf'=96,'sub'=8] {'leaf'}, use_global_device_ids=true, to_apply=%add.6 | all-reduce | flops 6144 | bytes 24576
  1621.2 90.7 %all-gather.11 = bf16[8,4,64]{2,1,0:T(4,128)(2,1)S(1)} all-gather(bf16[1,4,64]{2,1,0:T(4,128)(2,1)S(1)} %convert_bitcast_fusion.9), channel_id=1, replica_groups=mesh['leaf'=96,'sub'=8] {'sub'}, dimensions={0}, use_global_device_ids=true | all-gather | bytes 4608 | tf_op jit(solution)/shard_map/all_gather | solution.py:50
  1712.9 1.9 broadcast_select_fusion.1
  1714.8 1.4 scatter.24
  1718.0 2.0 pad_maximum_fusion.5
  1720.0 108.0 %all-reduce.7 = (f32[]{:T(128)}, f32[3]{0:T(128)S(1)}) all-reduce(f32[]{:T(128)} %get-tuple-element.83, f32[3]{0:T(128)S(1)} %pad_maximum_fusion.5), channel_id=1, replica_groups=mesh['leaf'=96,'sub'=8] {'leaf','sub'}, use_global_device_ids=true, to_apply=%region_20.0 | all-reduce | flops 4 | bytes 32 | tf_op jit(solution)/shard_map/psum | solution.py:115
  1831.2 2.0 broadcast_select_fusion
  1835.3 1.9 divide_bitcast_fusion
  (151 shorter events, 34.7 us)
Async XLA Ops:
  0.6 584.0 %copy-start = (bf16[4,2,256,256]{3,2,1,0:T(8,128)(2,1)S(1)}, bf16[4,2,256,256]{3,2,1,0:T(8,128)(2,1)}, u32[]{:S(2)}) copy-start(bf16[4,2,256,256]{3,2,1,0:T(8,128)(2,1)} %param.23) | copy-start | bytes 3145732
  2.0 121.1 %copy-start.2 = (f32[4,256]{1,0:T(4,128)S(1)}, f32[4,256]{1,0:T(4,128)}, u32[]{:S(2)}) copy-start(f32[4,256]{1,0:T(4,128)} %param.22) | copy-start | bytes 12292
  134.9 449.1 %collective-permute-start.1 = (bf16[32,256]{1,0:T(8,128)(2,1)S(1)}, bf16[32,256]{1,0:T(8,128)(2,1)S(1)}, u32[]{:S(2)}, u32[]{:S(2)}) collective-permute-start(bf16[32,256]{1,0:T(8,128)(2,1)S(1)} %reshape.327), channel_id=1, source_target_pairs={{8,0},{16,8},{24,16},{32,24},{40,32},{48,40},{56,48},{64,56},{72,6... | collective-permute-start | bytes 49160 | tf_op jit(solution)/shard_map/ppermute | solution.py:19
  136.2 447.8 %collective-permute-start = (bf16[32,256]{1,0:T(8,128)(2,1)S(1)}, bf16[32,256]{1,0:T(8,128)(2,1)S(1)}, u32[]{:S(2)}, u32[]{:S(2)}) collective-permute-start(bf16[32,256]{1,0:T(8,128)(2,1)S(1)} %reshape.327), channel_id=1, source_target_pairs={{0,8},{8,16},{16,24},{24,32},{32,40},{40,48},{48,56},{56,64},{64,7... | collective-permute-start | bytes 49160 | tf_op jit(solution)/shard_map/ppermute | solution.py:17
  140.2 1.2 copy-start.3
  141.4 0.7 copy-start.7
  487.5 0.7 copy-start.9
  487.6 0.8 copy-start.6
  488.5 91.1 %copy-start.4 = (s32[4,2]{0,1:T(2,128)S(1)}, s32[4,2]{0,1:T(2,128)}, u32[]{:S(2)}) copy-start(s32[4,2]{0,1:T(2,128)} %param.25) | copy-start | bytes 100
  488.7 92.1 %copy-start.1 = (bf16[4,64,256]{2,1,0:T(8,128)(2,1)S(1)}, bf16[4,64,256]{2,1,0:T(8,128)(2,1)}, u32[]{:S(2)}) copy-start(bf16[4,64,256]{2,1,0:T(8,128)(2,1)} %param.26) | copy-start | bytes 393220
  488.8 91.8 %copy-start.5 = (bf16[4,64,128]{2,1,0:T(8,128)(2,1)S(1)}, bf16[4,64,128]{2,1,0:T(8,128)(2,1)}, u32[]{:S(2)}) copy-start(bf16[4,64,128]{2,1,0:T(8,128)(2,1)} %param.27) | copy-start | bytes 196612
  580.7 0.7 copy-start.8
  581.4 0.7 copy-start.10
  705.8 439.9 %collective-permute-start.3 = (bf16[32,256]{1,0:T(8,128)(2,1)S(1)}, bf16[32,256]{1,0:T(8,128)(2,1)S(1)}, u32[]{:S(2)}, u32[]{:S(2)}) collective-permute-start(bf16[32,256]{1,0:T(8,128)(2,1)S(1)} %reshape.331), channel_id=1, source_target_pairs={{8,0},{16,8},{24,16},{32,24},{40,32},{48,40},{56,48},{64,56},{72,6... | collective-permute-start | bytes 49160 | tf_op jit(solution)/shard_map/ppermute | solution.py:19
  707.1 438.7 %collective-permute-start.2 = (bf16[32,256]{1,0:T(8,128)(2,1)S(1)}, bf16[32,256]{1,0:T(8,128)(2,1)S(1)}, u32[]{:S(2)}, u32[]{:S(2)}) collective-permute-start(bf16[32,256]{1,0:T(8,128)(2,1)S(1)} %reshape.331), channel_id=1, source_target_pairs={{0,8},{8,16},{16,24},{24,32},{32,40},{40,48},{48,56},{56,64},{64,7... | collective-permute-start | bytes 49160 | tf_op jit(solution)/shard_map/ppermute | solution.py:17
  1273.1 443.2 %collective-permute-start.5 = (bf16[32,256]{1,0:T(8,128)(2,1)S(1)}, bf16[32,256]{1,0:T(8,128)(2,1)S(1)}, u32[]{:S(2)}, u32[]{:S(2)}) collective-permute-start(bf16[32,256]{1,0:T(8,128)(2,1)S(1)} %reshape.335), channel_id=1, source_target_pairs={{8,0},{16,8},{24,16},{32,24},{40,32},{48,40},{56,48},{64,56},{72,6... | collective-permute-start | bytes 49160 | tf_op jit(solution)/shard_map/ppermute | solution.py:19
  1274.4 441.9 %collective-permute-start.4 = (bf16[32,256]{1,0:T(8,128)(2,1)S(1)}, bf16[32,256]{1,0:T(8,128)(2,1)S(1)}, u32[]{:S(2)}, u32[]{:S(2)}) collective-permute-start(bf16[32,256]{1,0:T(8,128)(2,1)S(1)} %reshape.335), channel_id=1, source_target_pairs={{0,8},{8,16},{16,24},{24,32},{32,40},{40,48},{48,56},{56,64},{64,7... | collective-permute-start | bytes 49160 | tf_op jit(solution)/shard_map/ppermute | solution.py:17
where the time goes:
time: 1840 us
  blocking collectives  1770 us (96%)
    unnamed x6, blocking collectives  1020 us
    psum x3, blocking collectives, per_device(): lax.psum((partial_dots, jnp.sum(image * image)), ('leaf', 'sub'))  321 us
    all_gather x3, blocking collectives, apply_matrix(): lax.all_gather(coef_bf, 'sub', axis=0, tiled=True)  272 us
    psum x1, blocking collectives, per_device(): start_sum = lax.psum(jnp.sum(start_vec * start_vec), ('leaf', 'sub'))  120 us
  transfers between devices with their start and end apart: 6, of which 0 were waited for; matrix products, arithmetic and copies ran while one was open for 1% of the time, Pallas kernels for 0%

commit v1 on v0

v1 whole, which is shorter than its diff:
```python
import functools

import jax
import jax.numpy as jnp
from jax import lax
from jax.experimental import pallas as pl
from jax.experimental.pallas import tpu as pltpu
from jax.sharding import PartitionSpec as P

MESH = pl.DeviceIdType.MESH
F32 = jnp.float32
BF16 = jnp.bfloat16
STEPS = 3
RING = 8


def dot_nt(a, b):
    return lax.dot_general(a, b, (((1,), (1,)), ((), ())), preferred_element_type=F32)


def dot_nn(a, b):
    return lax.dot_general(a, b, (((1,), (0,)), ((), ())), preferred_element_type=F32)


def split(x):
    high = x.astype(BF16).astype(F32)
    return jnp.concatenate([high, x - high], axis=0).astype(BF16)


def outward(j, n):
    half = (j + 1) // 2
    return n // 2 + half - 2 * half * (j % 2)


def kernel(
    nl,
    ns,
    ny,
    near_ids,
    far_ids,
    top_ids,
    start_h,
    near_h,
    lb_h,
    lc_h,
    nt_h,
    bt_h,
    tc_h,
    basis_ref,
    hess_ref,
    start_v,
    near_v,
    lb_v,
    lc_v,
    nt_v,
    bt_v,
    tc_v,
    t_v,
    r1_0,
    r1_1,
    r1_2,
    r1_3,
    r2_0,
    r2_1,
    r2_2,
    r2_3,
    x_0,
    x_1,
    x_2,
    c_0,
    c_1,
    c_2,
    in_sem,
    r1_send,
    r1_recv,
    r2_send,
    r2_recv,
    x_send,
    x_recv,
    c_send,
    c_recv,
):
    leaf, sub = lax.axis_index("leaf"), lax.axis_index("sub")
    r1, r2 = (r1_0, r1_1, r1_2, r1_3), (r2_0, r2_1, r2_2, r2_3)
    xall, call = (x_0, x_1, x_2), (c_0, c_1, c_2)
    nz = nl // ny
    z, y = leaf // ny, leaf % ny
    pairs = (
        (start_h, start_v),
        (bt_h, bt_v),
        (nt_h, nt_v),
        (lb_h, lb_v),
        (tc_h, tc_v),
        (lc_h, lc_v),
        (near_h, near_v),
    )
    loads = [pltpu.make_async_copy(s, d, in_sem.at[i]) for i, (s, d) in enumerate(pairs)]
    for load in loads:
        load.start()

    def branch_at(j):
        dz, dy = outward(j // ny, nz), outward(j % ny, ny)
        return lax.rem(z + dz, nz) * ny + lax.rem(y + dy, ny)

    barrier = pltpu.get_barrier_semaphore()

    def greet_branch(j, c):
        pl.semaphore_signal(
            barrier, inc=1, device_id=(branch_at(j), sub), device_id_type=MESH
        )
        return c

    def halo_at(j):
        side = j // ns
        back = 3 * (side // 2)
        to = lax.rem(leaf + side - back + nl, nl)
        return to, lax.rem(sub + j, ns), 1 - side + back

    def greet_halo(j, c):
        to, other, _ = halo_at(j)
        pl.semaphore_signal(barrier, inc=1, device_id=(to, other), device_id_type=MESH)
        return c

    lax.fori_loop(1, 3 * ns, greet_halo, 0)
    lax.fori_loop(0, nl - 1, greet_branch, 0)

    row4 = lax.broadcasted_iota(jnp.int32, (4, 256), 0)
    row8 = lax.broadcasted_iota(jnp.int32, (8, 256), 0)
    lane = lax.broadcasted_iota(jnp.int32, (1, 128), 1)
    total = float(nl * ns * 4 * 256)

    for load in loads[:4]:
        load.wait()
    up = dot_nn(bt_v[0], nt_v[0]).astype(BF16)
    for leaf_i in range(4):
        t_v[:, 256 * leaf_i : 256 * (leaf_i + 1)] = dot_nn(
            up[:, 64 * leaf_i : 64 * (leaf_i + 1)], lb_v[leaf_i]
        ).astype(BF16)

    def fold(p):
        s = jnp.sum(p, axis=0, keepdims=True) * (1.0 / total)
        s = s[:, :128] + s[:, 128:]
        return s + pltpu.roll(s, 64, 1)

    def term_of(x8):
        x8f = x8.astype(F32)
        parts = [jnp.where(row8 % 4 == i, x8f, 0.0).astype(BF16) for i in range(4)]
        out = dot_nt(jnp.concatenate(parts, axis=1), t_v[...])
        return jnp.sum(out, axis=0, keepdims=True)

    def send_r1(k):
        def go(j, c):
            pltpu.make_async_remote_copy(
                r1[k].at[sub],
                r1[k].at[sub],
                r1_send.at[k],
                r1_recv.at[k],
                device_id=(leaf, lax.rem(sub + j, ns)),
                device_id_type=MESH,
            ).start()
            return c

        lax.fori_loop(1, ns, go, 0)

    def bytes_wait(ref, sem):
        pltpu.make_async_copy(ref, ref, sem).wait()

    def send_r2(k):
        def go(j, c):
            pltpu.make_async_remote_copy(
                r2[k].at[leaf],
                r2[k].at[leaf],
                r2_send.at[k],
                r2_recv.at[k],
                device_id=(branch_at(j), sub),
                device_id_type=MESH,
            ).start()
            return c

        lax.fori_loop(0, nl - 1, go, 0)

    def sum_r1(k):
        bytes_wait(r1[k].at[pl.ds(0, ns - 1)], r1_recv.at[k])
        for row in range(2):
            acc = r1[k][0, row]
            for j in range(1, ns):
                acc = acc + r1[k][j, row]
            r2[k][leaf, row] = acc

    def send_x(k):
        def go(j, c):
            to, other, slot = halo_at(j)
            pltpu.make_async_remote_copy(
                xall[k].at[ns + sub],
                xall[k].at[slot * ns + sub],
                x_send.at[k],
                x_recv.at[k],
                device_id=(to, other),
                device_id_type=MESH,
            ).start()
            return c

        lax.fori_loop(1, 3 * ns, go, 0)

    def send_c(k):
        def go(j, c):
            pltpu.make_async_remote_copy(
                call[k].at[sub],
                call[k].at[sub],
                c_send.at[k],
                c_recv.at[k],
                device_id=(leaf, lax.rem(sub + j, ns)),
                device_id_type=MESH,
            ).start()
            return c

        lax.fori_loop(1, ns, go, 0)

    def store_coef(k, x8):
        out = dot_nt(x8, lb_v[...].reshape(256, 256))
        out = out[:4] + out[4:]
        for i in range(4):
            piece = out[i : i + 1, 128 * (i // 2) : 128 * (i // 2) + 128]
            piece = jnp.where((lane // 64) == i % 2, piece, 0.0)
            call[k][sub, i] = piece + pltpu.roll(piece, 64, 1)

    def local_part(k, x8):
        bytes_wait(xall[k].at[pl.ds(0, 3 * ns - 1)], x_recv.at[k])
        bytes_wait(call[k].at[pl.ds(0, ns - 1)], c_recv.at[k])
        near_rows, far_rows = [], []
        for i in range(4):
            one = near_ids[i, 0]
            outside = jnp.logical_or(
                jnp.logical_and(leaf == 0, one < 4 * ns),
                jnp.logical_and(leaf == nl - 1, one >= 8 * ns),
            )
            keep = jnp.where(outside, 0.0, 1.0)
            near_rows.append(xall[k][one // 4, one % 4] * keep)
            first, second = far_ids[i, 0], far_ids[i, 1]
            far_rows.append(
                jnp.where(
                    lane < 64,
                    call[k][first // 4, first % 4],
                    call[k][second // 4, second % 4],
                )
            )
        p8 = split(jnp.concatenate(near_rows, axis=0))
        f8 = split(jnp.concatenate(far_rows, axis=0))
        out = jnp.zeros((4, 256), F32)
        for i in range(4):
            o8 = dot_nt(x8, near_v[i, 0]) + dot_nt(p8, near_v[i, 1])
            g8 = dot_nt(f8, lc_v[i])
            o4 = o8[:4] + o8[4:] + dot_nn((g8[:4] + g8[4:]).astype(BF16), lb_v[i])
            out = jnp.where(row4 == i, o4, out)
        return out

    def dots_total(k, row):
        acc = jnp.zeros((1, 128), F32)
        for c in range(0, nl, min(nl, 8)):
            acc = acc + jnp.sum(r2[k][pl.ds(c, min(nl, 8)), row], axis=0)
        return acc

    def half_sum(v, half):
        return jnp.sum(jnp.where((lane // 64) == half, v, 0.0), axis=1, keepdims=True)

    us = [start_v[...]]
    gram = {}
    nus = []
    halves = [None, None]
    for k in range(STEPS):
        x = us[k]
        x8 = split(x)
        term = term_of(x8)
        term = jnp.concatenate([term, term], axis=1)
        r1[k][sub, 0] = jnp.where(lane < 64, term, fold(x * x))
        if k == 0:
            r1[k][sub, 1] = jnp.zeros((1, 128), F32)
        else:
            r1[k][sub, 1] = jnp.where(lane < 64, fold(x * us[0]), fold(x * us[(k == 2) * 1]))
        if k == 0:
            pl.semaphore_wait(barrier, nl - 1 + 3 * ns - 1)
        send_r1(k)
        for i in range(4):
            xall[k][ns + sub, i] = x[i : i + 1]
        send_x(k)
        store_coef(k, x8)
        send_c(k)
        sum_r1(k)
        bytes_wait(xall[k].at[pl.ds(0, 3 * ns - 1)], x_send.at[k])
        bytes_wait(call[k].at[pl.ds(0, ns - 1)], c_send.at[k])
        send_r2(k)
        if k == 0:
            for load in loads[4:]:
                load.wait()
        local = local_part(k, x8)
        bytes_wait(r2[k].at[pl.ds(0, nl - 1)], r2_recv.at[k])
        picked = [r2[k][top_ids[0, s], 0] for s in range(4)]
        pair0 = jnp.where(lane < 64, picked[0], pltpu.roll(picked[1], 64, 1))
        pair1 = jnp.where(lane < 64, picked[2], pltpu.roll(picked[3], 64, 1))
        chosen = split(jnp.concatenate([pair0, pair1], axis=1))
        branchl = jnp.sum(dot_nt(chosen, tc_v[0]), axis=0, keepdims=True)
        down = jnp.sum(dot_nn(split(branchl), t_v[...]), axis=0, keepdims=True)
        down = jnp.concatenate([down[:, 256 * i : 256 * (i + 1)] for i in range(4)], axis=0)
        sums = dots_total(k, 0)
        gram[k, k] = half_sum(sums, 1)
        if k >= 1:
            sums = dots_total(k, 1)
            gram[k, 0] = half_sum(sums, 0)
            if k == 2:
                gram[k, 1] = half_sum(sums, 1)
        guarded = jnp.maximum(gram[k, k], 1e-30)
        nus.append(jnp.sqrt(guarded))
        us.append((local + down) * lax.rsqrt(guarded))

    x = us[3]
    r1[3][sub, 0] = jnp.where(lane < 64, fold(x * us[2]), fold(x * x))
    r1[3][sub, 1] = jnp.where(lane < 64, fold(x * us[0]), fold(x * us[1]))
    send_r1(3)

    def g(i, j):
        return gram[max(i, j), min(i, j)]

    zero = jnp.zeros((1, 1), F32)
    coefs = [[lax.rsqrt(gram[0, 0] + 1e-06)]]
    basis_ref[0] = us[0] * coefs[0][0]
    hess = {}

    def column(j):
        a = coefs[j]
        w = []
        for i in range(j + 2):
            v = zero
            if i <= j:
                v = v + 0.5 * a[i]
            if i >= 1:
                v = v + nus[i - 1] * a[i - 1]
            w.append(v)
        gw = [sum((g(i, m) * w[m] for m in range(1, j + 2)), g(i, 0) * w[0]) for i in range(j + 2)]
        square = sum((w[i] * gw[i] for i in range(1, j + 2)), w[0] * gw[0])
        remain = square
        new = list(w)
        for i in range(j + 1):
            h = sum((coefs[i][m] * gw[m] for m in range(1, i + 1)), coefs[i][0] * gw[0])
            hess[i, j] = h
            remain = remain - h * h
            for m in range(i + 1):
                new[m] = new[m] - h * coefs[i][m]
        scale = jnp.sqrt(jnp.maximum(remain, 0.01 * square))
        hess[j + 1, j] = scale
        inverse = 1.0 / scale
        coefs.append([v * inverse for v in new])

    def store_basis(j):
        acc = us[0] * coefs[j][0]
        for m in range(1, j + 1):
            acc = acc + us[m] * coefs[j][m]
        basis_ref[j] = acc

    column(0)
    column(1)
    store_basis(1)
    store_basis(2)
    sum_r1(3)
    send_r2(3)
    bytes_wait(r2[3].at[pl.ds(0, nl - 1)], r2_recv.at[3])
    sums = dots_total(3, 0)
    gram[3, 2], gram[3, 3] = half_sum(sums, 0), half_sum(sums, 1)
    sums = dots_total(3, 1)
    gram[3, 0], gram[3, 1] = half_sum(sums, 0), half_sum(sums, 1)
    column(2)
    store_basis(3)
    rows = lax.broadcasted_iota(jnp.int32, (4, 3), 0)
    cols = lax.broadcasted_iota(jnp.int32, (4, 3), 1)
    table = jnp.zeros((4, 3), F32)
    for (i, j), h in hess.items():
        table = jnp.where(jnp.logical_and(rows == i, cols == j), h, table)
    hess_ref[...] = table

    for k in range(4):
        bytes_wait(r1[k].at[pl.ds(0, ns - 1)], r1_send.at[k])
        bytes_wait(r2[k].at[pl.ds(0, nl - 1)], r2_send.at[k])


def solution(mesh):
    nl, ns = mesh.shape["leaf"], mesh.shape["sub"]
    ny = RING if nl % RING == 0 else 1

    def per_device(
        start_vec,
        near_blocks,
        near_ids,
        far_ids,
        leaf_basis,
        leaf_coupling,
        node_transfer,
        branch_transfer,
        top_ids,
        top_coupling,
    ):
        smem = pl.BlockSpec(memory_space=pltpu.SMEM)
        hbm = pl.BlockSpec(memory_space=pl.ANY)
        vmem = pl.BlockSpec(memory_space=pltpu.VMEM)
        dma = pltpu.SemaphoreType.DMA
        return pl.pallas_call(
            functools.partial(kernel, nl, ns, ny),
            out_shape=(
                jax.ShapeDtypeStruct((4, 4, 256), F32),
                jax.ShapeDtypeStruct((4, 3), F32),
            ),
            in_specs=[smem] * 3 + [hbm] * 7,
            out_specs=(vmem, vmem),
            scratch_shapes=[
                pltpu.VMEM((4, 256), F32),
                pltpu.VMEM((4, 2, 256, 256), BF16),
                pltpu.VMEM((4, 64, 256), BF16),
                pltpu.VMEM((4, 64, 128), BF16),
                pltpu.VMEM((1, 64, 256), BF16),
                pltpu.VMEM((1, 64, 64), BF16),
                pltpu.VMEM((1, 64, 256), BF16),
                pltpu.VMEM((64, 1024), BF16),
                *[pltpu.VMEM((ns, 2, 1, 128), F32)] * 4,
                *[pltpu.VMEM((nl, 2, 1, 128), F32)] * 4,
                *[pltpu.VMEM((3 * ns, 4, 1, 256), F32)] * 3,
                *[pltpu.VMEM((ns, 4, 1, 128), F32)] * 3,
                dma((7,)),
                dma((4,)),
                dma((4,)),
                dma((4,)),
                dma((4,)),
                dma((3,)),
                dma((3,)),
                dma((3,)),
                dma((3,)),
            ],
            compiler_params=pltpu.CompilerParams(
                collective_id=0, has_side_effects=True, vmem_limit_bytes=40 * 2**20
            ),
        )(
            near_ids,
            far_ids,
            top_ids,
            start_vec,
            near_blocks,
            leaf_basis,
            leaf_coupling,
            node_transfer,
            branch_transfer,
            top_coupling,
        )

    placed = (
        P(("leaf", "sub"), None),
        P(("leaf", "sub"), None, None, None),
        P(("leaf", "sub"), None),
        P(("leaf", "sub"), None),
        P(("leaf", "sub"), None, None),
        P(("leaf", "sub"), None, None),
        P(("leaf", "sub"), None, None),
        P(("leaf", "sub"), None, None),
        P("leaf", None),
        P("leaf", None, None),
    )
    return jax.shard_map(
        per_device,
        mesh=mesh,
        in_specs=placed,
        out_specs=(P(None, ("leaf", "sub"), None), P()),
        check_vma=False,
    )
```

time: 1840 us -> 84.3 us (0.05)
  blocking collectives: 1770 us -> 0 us
  Pallas kernels: 0 us -> 75.4 us
    unnamed x6 -> x0, blocking collectives: 1020 us -> none
    psum x4 -> x0, blocking collectives: 442 us -> none  [the longest x3 321 us: per_device(): lax.psum((partial_dots, jnp.sum(image * image)), ('leaf', 'sub'))]
    all_gather x6 -> x0, blocking collectives: 307 us -> none  [the longest x3 272 us: apply_matrix(): lax.all_gather(coef_bf, 'sub', axis=0, tiled=True)]
    pallas_call x0 -> x1, Pallas kernels: none -> 75.4 us  [per_device(): pl.pallas_call(functools.partial(kernel, nl, ns, ny), out_shape=(jax.Shap...]
  transfers between devices with their start and end apart: 6 -> 0, of which waited for: 0 -> 0; matrix products, arithmetic and copies ran while one was open for 1% -> 0% of each run, Pallas kernels for 0% -> 0%
where the time goes in v1:
time: 84.3 us; the launch traced here: 83.8 us
  Pallas kernels  75.4 us (89%)
  local copies, waits for them, and re-layouts  7.8 us (9%)
    pallas_call x1, Pallas kernels, per_device(): pl.pallas_call(functools.partial(kernel, nl, ns, ny), out_shape=(jax.Shap...  75.4 us
    unnamed x22, local copies, waits for them, and re-layouts  7.8 us

profile of v1, /device:TPU:1, one launch (start us, length us, event | category | flops | bytes accessed | tf_op | source)
XLA Modules:
  0.0 83.8 jit_solution(14398001279269106243)
XLA Ops:
  0.6 0.0 copy-start.8
  0.6 0.0 copy-start.6
  0.6 0.8 copy.12.near_ids
  1.4 0.0 copy-done.8
  1.4 0.0 copy-start.7
  1.4 0.1 copy.13.far_ids
  1.5 0.0 copy-done.6
  1.5 0.6 copy-done.7
  2.1 0.0 copy-start
  2.1 1.2 %copy-done = bf16[4,2,256,256]{3,2,1,0:T(8,128)(2,1)S(1)} copy-done((bf16[4,2,256,256]{3,2,1,0:T(8,128)(2,1)S(1)}, bf16[4,2,256,256]{3,2,1,0:T(8,128)(2,1)}, u32[]{:S(2)}) %copy-start) | copy-done | bytes 1048600
  3.3 0.0 copy-start.1
  3.3 0.9 %copy-done.1 = bf16[4,64,256]{2,1,0:T(8,128)(2,1)S(1)} copy-done((bf16[4,64,256]{2,1,0:T(8,128)(2,1)S(1)}, bf16[4,64,256]{2,1,0:T(8,128)(2,1)}, u32[]{:S(2)}) %copy-start.1) | copy-done | bytes 131096
  4.2 0.0 copy-start.2
  4.2 0.8 copy-done.2
  5.0 0.0 copy-start.3
  5.0 0.8 copy-done.3
  5.8 0.0 copy-start.4
  5.8 0.8 copy-done.4
  6.5 0.0 copy-start.5
  6.6 0.7 copy-done.5
  7.3 75.4 %shard_map.113 = (f32[4,4,256]{2,1,0:T(4,128)S(1)}, f32[4,3]{1,0:T(4,128)S(1)}) custom-call(s32[4,1]{1,0:T(4,128)S(1)} %copy.12.near_ids, s32[4,2]{1,0:T(4,128)S(1)} %copy.13.far_ids, s32[1,4]{1,0:T(1,128)S(1)} %copy-done.7, f32[4,256]{1,0:T(4,128)S(1)} %copy-done.6, bf16[4,2,256,256]{3,2,1,0:T(8,128)(2,1)S(1)} %copy-done, ...), custom_call_target="tpu_custom_call" | custom-call | tf_op jit(solution)/shard_map/pallas_call | solution.py:404
  82.7 0.6 copy.16
  83.3 0.6 copy.17
Async XLA Ops:
  0.6 0.8 copy-start.8
  0.6 0.9 %copy-start.6 = (f32[4,256]{1,0:T(4,128)S(1)}, f32[4,256]{1,0:T(4,128)}, u32[]{:S(2)}) copy-start(f32[4,256]{1,0:T(4,128)} %start_h.1) | copy-start | bytes 12292
  1.4 0.7 copy-start.7
  2.1 1.2 %copy-start = (bf16[4,2,256,256]{3,2,1,0:T(8,128)(2,1)S(1)}, bf16[4,2,256,256]{3,2,1,0:T(8,128)(2,1)}, u32[]{:S(2)}) copy-start(bf16[4,2,256,256]{3,2,1,0:T(8,128)(2,1)} %near_h.1) | copy-start | bytes 3145732
  3.3 0.9 %copy-start.1 = (bf16[4,64,256]{2,1,0:T(8,128)(2,1)S(1)}, bf16[4,64,256]{2,1,0:T(8,128)(2,1)}, u32[]{:S(2)}) copy-start(bf16[4,64,256]{2,1,0:T(8,128)(2,1)} %lb_h.1) | copy-start | bytes 393220
  4.2 0.8 %copy-start.2 = (bf16[4,64,128]{2,1,0:T(8,128)(2,1)S(1)}, bf16[4,64,128]{2,1,0:T(8,128)(2,1)}, u32[]{:S(2)}) copy-start(bf16[4,64,128]{2,1,0:T(8,128)(2,1)} %lc_h.1) | copy-start | bytes 196612
  5.0 0.8 copy-start.3
  5.8 0.8 copy-start.4
  6.5 0.7 copy-start.5

commit v2 on v1

--- a/solution.py
+++ b/solution.py
@@ -36,9 +36,9 @@
     nl,
     ns,
     ny,
-    near_ids,
-    far_ids,
-    top_ids,
+    near_ids_h,
+    far_ids_h,
+    top_ids_h,
     start_h,
     near_h,
     lb_h,
@@ -48,6 +48,9 @@
     tc_h,
     basis_ref,
     hess_ref,
+    near_ids,
+    far_ids,
+    top_ids,
     start_v,
     near_v,
     lb_v,
@@ -56,6 +59,8 @@
     bt_v,
     tc_v,
     t_v,
+    tcw_v,
+    gram_v,
     r1_0,
     r1_1,
     r1_2,
@@ -79,6 +84,8 @@
     x_recv,
     c_send,
     c_recv,
+    g_send,
+    g_recv,
 ):
     leaf, sub = lax.axis_index("leaf"), lax.axis_index("sub")
     r1, r2 = (r1_0, r1_1, r1_2, r1_3), (r2_0, r2_1, r2_2, r2_3)
@@ -93,22 +100,31 @@
         (tc_h, tc_v),
         (lc_h, lc_v),
         (near_h, near_v),
+        (near_ids_h, near_ids),
+        (far_ids_h, far_ids),
+        (top_ids_h, top_ids),
     )
     loads = [pltpu.make_async_copy(s, d, in_sem.at[i]) for i, (s, d) in enumerate(pairs)]
     for load in loads:
         load.start()
 
-    def branch_at(j):
-        dz, dy = outward(j // ny, nz), outward(j % ny, ny)
-        return lax.rem(z + dz, nz) * ny + lax.rem(y + dy, ny)
+    columns = [lax.rem(y + outward(j, ny), ny) for j in range(ny)]
+
+    def each_branch(act):
+        def ring(j, c):
+            row = lax.rem(z + outward(j, nz), nz) * ny
+            for column in columns:
+                act(row + column)
+            return c
+
+        lax.fori_loop(0, nz - 1, ring, 0)
+        for column in columns[:-1]:
+            act(z * ny + column)
 
     barrier = pltpu.get_barrier_semaphore()
 
-    def greet_branch(j, c):
-        pl.semaphore_signal(
-            barrier, inc=1, device_id=(branch_at(j), sub), device_id_type=MESH
-        )
-        return c
+    def greet_branch(to):
+        pl.semaphore_signal(barrier, inc=1, device_id=(to, sub), device_id_type=MESH)
 
     def halo_at(j):
         side = j // ns
@@ -121,8 +137,8 @@
         pl.semaphore_signal(barrier, inc=1, device_id=(to, other), device_id_type=MESH)
         return c
 
+    each_branch(greet_branch)
     lax.fori_loop(1, 3 * ns, greet_halo, 0)
-    lax.fori_loop(0, nl - 1, greet_branch, 0)
 
     row4 = lax.broadcasted_iota(jnp.int32, (4, 256), 0)
     row8 = lax.broadcasted_iota(jnp.int32, (8, 256), 0)
@@ -146,7 +162,8 @@
         x8f = x8.astype(F32)
         parts = [jnp.where(row8 % 4 == i, x8f, 0.0).astype(BF16) for i in range(4)]
         out = dot_nt(jnp.concatenate(parts, axis=1), t_v[...])
-        return jnp.sum(out, axis=0, keepdims=True)
+        out = jnp.sum(out, axis=0, keepdims=True)
+        return jnp.concatenate([out, out], axis=1)
 
     def send_r1(k):
         def go(j, c):
@@ -166,26 +183,41 @@
         pltpu.make_async_copy(ref, ref, sem).wait()
 
     def send_r2(k):
-        def go(j, c):
+        def go(to):
             pltpu.make_async_remote_copy(
                 r2[k].at[leaf],
                 r2[k].at[leaf],
                 r2_send.at[k],
                 r2_recv.at[k],
-                device_id=(branch_at(j), sub),
+                device_id=(to, sub),
+                device_id_type=MESH,
+            ).start()
+
+        each_branch(go)
+
+    def branch_sum(k):
+        bytes_wait(r1[k].at[pl.ds(0, ns - 1)], r1_recv.at[k])
+        sums = []
+        for row in range(3):
+            acc = r1[k][0, row]
+            for j in range(1, ns):
+                acc = acc + r1[k][j, row]
+            sums.append(acc)
+        return sums
+
+    def send_gram():
+        def go(j, c):
+            pltpu.make_async_remote_copy(
+                gram_v.at[sub],
+                gram_v.at[sub],
+                g_send,
+                g_recv,
+                device_id=(leaf, lax.rem(sub + j, ns)),
                 device_id_type=MESH,
             ).start()
             return c
 
-        lax.fori_loop(0, nl - 1, go, 0)
-
-    def sum_r1(k):
-        bytes_wait(r1[k].at[pl.ds(0, ns - 1)], r1_recv.at[k])
-        for row in range(2):
-            acc = r1[k][0, row]
-            for j in range(1, ns):
-                acc = acc + r1[k][j, row]
-            r2[k][leaf, row] = acc
+        lax.fori_loop(1, ns, go, 0)
 
     def send_x(k):
         def go(j, c):
@@ -224,19 +256,26 @@
             piece = jnp.where((lane // 64) == i % 2, piece, 0.0)
             call[k][sub, i] = piece + pltpu.roll(piece, 64, 1)
 
-    def local_part(k, x8):
+    def own_part(x8):
+        out = jnp.zeros((4, 256), F32)
+        for i in range(4):
+            o8 = dot_nt(x8, near_v[i, 0])
+            out = jnp.where(row4 == i, o8[:4] + o8[4:], out)
+        return out
+
+    def partner_part(k):
         bytes_wait(xall[k].at[pl.ds(0, 3 * ns - 1)], x_recv.at[k])
         bytes_wait(call[k].at[pl.ds(0, ns - 1)], c_recv.at[k])
         near_rows, far_rows = [], []
         for i in range(4):
-            one = near_ids[i, 0]
+            one = near_ids[0, i]
             outside = jnp.logical_or(
                 jnp.logical_and(leaf == 0, one < 4 * ns),
                 jnp.logical_and(leaf == nl - 1, one >= 8 * ns),
             )
             keep = jnp.where(outside, 0.0, 1.0)
             near_rows.append(xall[k][one // 4, one % 4] * keep)
-            first, second = far_ids[i, 0], far_ids[i, 1]
+            first, second = far_ids[0, i], far_ids[1, i]
             far_rows.append(
                 jnp.where(
                     lane < 64,
@@ -248,74 +287,127 @@
         f8 = split(jnp.concatenate(far_rows, axis=0))
         out = jnp.zeros((4, 256), F32)
         for i in range(4):
-            o8 = dot_nt(x8, near_v[i, 0]) + dot_nt(p8, near_v[i, 1])
+            o8 = dot_nt(p8, near_v[i, 1])
             g8 = dot_nt(f8, lc_v[i])
             o4 = o8[:4] + o8[4:] + dot_nn((g8[:4] + g8[4:]).astype(BF16), lb_v[i])
             out = jnp.where(row4 == i, o4, out)
         return out
 
-    def dots_total(k, row):
-        acc = jnp.zeros((1, 128), F32)
-        for c in range(0, nl, min(nl, 8)):
-            acc = acc + jnp.sum(r2[k][pl.ds(c, min(nl, 8)), row], axis=0)
+    def over_table(k, op):
+        step = min(nl, 8)
+        acc = None
+        for c in range(0, nl, step):
+            rows = r2[k][pl.ds(c, step)]
+            part = jnp.max(jnp.abs(rows), axis=0) if op == "max" else jnp.sum(rows, axis=0)
+            if acc is not None:
+                part = jnp.maximum(acc, part) if op == "max" else acc + part
+            acc = part
         return acc
 
     def half_sum(v, half):
         return jnp.sum(jnp.where((lane // 64) == half, v, 0.0), axis=1, keepdims=True)
 
-    us = [start_v[...]]
-    gram = {}
-    nus = []
-    halves = [None, None]
-    for k in range(STEPS):
-        x = us[k]
-        x8 = split(x)
-        term = term_of(x8)
-        term = jnp.concatenate([term, term], axis=1)
-        r1[k][sub, 0] = jnp.where(lane < 64, term, fold(x * x))
-        if k == 0:
-            r1[k][sub, 1] = jnp.zeros((1, 128), F32)
-        else:
-            r1[k][sub, 1] = jnp.where(lane < 64, fold(x * us[0]), fold(x * us[(k == 2) * 1]))
-        if k == 0:
-            pl.semaphore_wait(barrier, nl - 1 + 3 * ns - 1)
-        send_r1(k)
+    def exchange_leaves(k, x, x8):
         for i in range(4):
             xall[k][ns + sub, i] = x[i : i + 1]
         send_x(k)
         store_coef(k, x8)
         send_c(k)
-        sum_r1(k)
+
+    def leaves_sent(k):
         bytes_wait(xall[k].at[pl.ds(0, 3 * ns - 1)], x_send.at[k])
         bytes_wait(call[k].at[pl.ds(0, ns - 1)], c_send.at[k])
-        send_r2(k)
+
+    low = lane < 64
+    us = [start_v[...]]
+    x8 = split(us[0])
+    r1[0][sub, 0] = term_of(x8)
+    r1[0][sub, 1] = fold(us[0] * us[0])
+    r1[0][sub, 2] = jnp.zeros((1, 128), F32)
+    pl.semaphore_wait(barrier, nl - 1 + 3 * ns - 1)
+    send_r1(0)
+    exchange_leaves(0, us[0], x8)
+    both = dot_nt(t_v[...], t_v[...])
+    gram_v[sub] = jnp.concatenate([both, both], axis=1)
+    order = [(i, j) for i in range(4) for j in range(i + 1)]
+    pending = jnp.zeros((1, 128), F32)
+
+    def put(row, i, j, value):
+        return row + jnp.where(lane == order.index((i, j)), value, 0.0)
+
+    sums = branch_sum(0)
+    r2[0][leaf] = sums[0]
+    send_r2(0)
+    send_gram()
+    pending = put(pending, 0, 0, half_sum(sums[1], 0))
+    branchc = [sums[0]]
+    for load in loads[4:]:
+        load.wait()
+    before = jnp.ones((1, 1), F32)
+    nus = []
+    own = own_part(x8)
+    for k in range(STEPS):
+        local = own + partner_part(k)
+        r1[k + 1][sub, 0] = term_of(split(local))
+        dots = [fold(local * u) for u in us]
+        r1[k + 1][sub, 1] = jnp.where(low, fold(local * local), dots[0])
+        r1[k + 1][sub, 2] = jnp.where(low, dots[min(k, 1)], dots[k])
+        send_r1(k + 1)
         if k == 0:
-            for load in loads[4:]:
-                load.wait()
-        local = local_part(k, x8)
+            bytes_wait(gram_v.at[pl.ds(0, ns - 1)], g_recv)
+            whole = gram_v[0]
+            for j in range(1, ns):
+                whole = whole + gram_v[j]
+            both = dot_nn(whole[:, :64].astype(BF16), tc_v[0]).astype(BF16)
+            tcw_v[:64] = both
+            tcw_v[64:128] = both
+            tcw_v[128:192] = tc_v[0]
+            tcw_v[192:] = tc_v[0]
+        sums = branch_sum(k + 1)
         bytes_wait(r2[k].at[pl.ds(0, nl - 1)], r2_recv.at[k])
-        picked = [r2[k][top_ids[0, s], 0] for s in range(4)]
-        pair0 = jnp.where(lane < 64, picked[0], pltpu.roll(picked[1], 64, 1))
-        pair1 = jnp.where(lane < 64, picked[2], pltpu.roll(picked[3], 64, 1))
+        picked = [r2[k][top_ids[0, s]] for s in range(4)]
+        pair0 = jnp.where(low, picked[0], picked[1])
+        pair1 = jnp.where(low, picked[2], picked[3])
         chosen = split(jnp.concatenate([pair0, pair1], axis=1))
-        branchl = jnp.sum(dot_nt(chosen, tc_v[0]), axis=0, keepdims=True)
-        down = jnp.sum(dot_nn(split(branchl), t_v[...]), axis=0, keepdims=True)
+        got = dot_nt(chosen, tcw_v[...])
+        got = (got[:1] + got[1:]) * before
+        added, branchl = got[:, :128], got[:, 128:]
+        if k < 2:
+            later = sums[0] + added
+            r2[k + 1][leaf] = later
+            send_r2(k + 1)
+            biggest = jnp.max(over_table(k, "max"), axis=1, keepdims=True) * before
+            alpha = 1.0 / jnp.maximum(biggest, 1.0)
+        else:
+            alpha = jnp.full((1, 1), 2.0**-20, F32)
+        nus.append(1.0 / alpha)
+        scaled = branchl * (alpha * (1.0 / total))
+        factors = jnp.where(low, alpha * (2.0 * sums[0] + added), branchc[0])
+        first = sums[1] * jnp.where(low, alpha * alpha, alpha) + scaled * factors
+        pending = put(pending, k + 1, k + 1, half_sum(first, 0))
+        pending = put(pending, k + 1, 0, half_sum(first, 1))
+        if k >= 1:
+            second = sums[2] * alpha + scaled * jnp.where(low, branchc[1], branchc[k])
+            pending = put(pending, k + 1, 1, half_sum(second, 0))
+            if k == 2:
+                pending = put(pending, 3, 2, half_sum(second, 1))
+        if k == 2:
+            r2[3][leaf] = pending
+            send_r2(3)
+        down = jnp.sum(dot_nn(split(branchl[:, :64]), t_v[...]), axis=0, keepdims=True)
         down = jnp.concatenate([down[:, 256 * i : 256 * (i + 1)] for i in range(4)], axis=0)
-        sums = dots_total(k, 0)
-        gram[k, k] = half_sum(sums, 1)
-        if k >= 1:
-            sums = dots_total(k, 1)
-            gram[k, 0] = half_sum(sums, 0)
-            if k == 2:
-                gram[k, 1] = half_sum(sums, 1)
-        guarded = jnp.maximum(gram[k, k], 1e-30)
-        nus.append(jnp.sqrt(guarded))
-        us.append((local + down) * lax.rsqrt(guarded))
-
-    x = us[3]
-    r1[3][sub, 0] = jnp.where(lane < 64, fold(x * us[2]), fold(x * x))
-    r1[3][sub, 1] = jnp.where(lane < 64, fold(x * us[0]), fold(x * us[1]))
-    send_r1(3)
+        x = (local + down) * alpha
+        us.append(x)
+        if k < 2:
+            x8 = split(x)
+            exchange_leaves(k + 1, x, x8)
+            branchc.append(later * alpha)
+            before = alpha
+            own = own_part(x8)
+
+    bytes_wait(r2[3].at[pl.ds(0, nl - 1)], r2_recv.at[3])
+    sums = over_table(3, "sum")
+    gram = {ij: sums[:, i : i + 1] for i, ij in enumerate(order)}
 
     def g(i, j):
         return gram[max(i, j), min(i, j)]
@@ -356,19 +448,9 @@
             acc = acc + us[m] * coefs[j][m]
         basis_ref[j] = acc
 
-    column(0)
-    column(1)
-    store_basis(1)
-    store_basis(2)
-    sum_r1(3)
-    send_r2(3)
-    bytes_wait(r2[3].at[pl.ds(0, nl - 1)], r2_recv.at[3])
-    sums = dots_total(3, 0)
-    gram[3, 2], gram[3, 3] = half_sum(sums, 0), half_sum(sums, 1)
-    sums = dots_total(3, 1)
-    gram[3, 0], gram[3, 1] = half_sum(sums, 0), half_sum(sums, 1)
-    column(2)
-    store_basis(3)
+    for j in range(STEPS):
+        column(j)
+        store_basis(j + 1)
     rows = lax.broadcasted_iota(jnp.int32, (4, 3), 0)
     cols = lax.broadcasted_iota(jnp.int32, (4, 3), 1)
     table = jnp.zeros((4, 3), F32)
@@ -379,6 +461,9 @@
     for k in range(4):
         bytes_wait(r1[k].at[pl.ds(0, ns - 1)], r1_send.at[k])
         bytes_wait(r2[k].at[pl.ds(0, nl - 1)], r2_send.at[k])
+    for k in range(STEPS):
+        leaves_sent(k)
+    bytes_wait(gram_v.at[pl.ds(0, ns - 1)], g_send)
 
 
 def solution(mesh):
@@ -397,8 +482,7 @@
         top_ids,
         top_coupling,
     ):
-        smem = pl.BlockSpec(memory_space=pltpu.SMEM)
-        hbm = pl.BlockSpec(memory_space=pl.ANY)
+        hbm = pl.BlockSpec(memory_space=pltpu.HBM)
         vmem = pl.BlockSpec(memory_space=pltpu.VMEM)
         dma = pltpu.SemaphoreType.DMA
         return pl.pallas_call(
@@ -407,9 +491,12 @@
                 jax.ShapeDtypeStruct((4, 4, 256), F32),
                 jax.ShapeDtypeStruct((4, 3), F32),
             ),
-            in_specs=[smem] * 3 + [hbm] * 7,
+            in_specs=[hbm] * 10,
             out_specs=(vmem, vmem),
             scratch_shapes=[
+                pltpu.SMEM((1, 4), jnp.int32),
+                pltpu.SMEM((2, 4), jnp.int32),
+                pltpu.SMEM((1, 4), jnp.int32),
                 pltpu.VMEM((4, 256), F32),
                 pltpu.VMEM((4, 2, 256, 256), BF16),
                 pltpu.VMEM((4, 64, 256), BF16),
@@ -418,11 +505,13 @@
                 pltpu.VMEM((1, 64, 64), BF16),
                 pltpu.VMEM((1, 64, 256), BF16),
                 pltpu.VMEM((64, 1024), BF16),
-                *[pltpu.VMEM((ns, 2, 1, 128), F32)] * 4,
-                *[pltpu.VMEM((nl, 2, 1, 128), F32)] * 4,
+                pltpu.VMEM((256, 256), BF16),
+                pltpu.VMEM((ns, 64, 128), F32),
+                *[pltpu.VMEM((ns, 3, 1, 128), F32)] * 4,
+                *[pltpu.VMEM((nl, 1, 128), F32)] * 4,
                 *[pltpu.VMEM((3 * ns, 4, 1, 256), F32)] * 3,
                 *[pltpu.VMEM((ns, 4, 1, 128), F32)] * 3,
-                dma((7,)),
+                dma((10,)),
                 dma((4,)),
                 dma((4,)),
                 dma((4,)),
@@ -431,21 +520,28 @@
                 dma((3,)),
                 dma((3,)),
                 dma((3,)),
+                dma,
+                dma,
             ],
             compiler_params=pltpu.CompilerParams(
                 collective_id=0, has_side_effects=True, vmem_limit_bytes=40 * 2**20
             ),
         )(
-            near_ids,
-            far_ids,
-            top_ids,
-            start_vec,
-            near_blocks,
-            leaf_basis,
-            leaf_coupling,
-            node_transfer,
-            branch_transfer,
-            top_coupling,
+            *(
+                pltpu.with_memory_space_constraint(v, pltpu.HBM)
+                for v in (
+                    near_ids.T,
+                    far_ids.T,
+                    top_ids,
+                    start_vec,
+                    near_blocks,
+                    leaf_basis,
+                    leaf_coupling,
+                    node_transfer,
+                    branch_transfer,
+                    top_coupling,
+                )
+            )
         )
 
     placed = (

time: 84.3 us -> 64.7 us (0.77)
  Pallas kernels: 75.4 us -> 62.8 us
  local copies, waits for them, and re-layouts: 7.8 us -> 1.19 us
    pallas_call x1, Pallas kernels: 75.4 us -> 62.8 us  [per_device(): pl.pallas_call(functools.partial(kernel, nl, ns, ny), out_shape=(jax.Shap...]
    unnamed x22 -> x2, local copies, waits for them, and re-layouts: 7.8 us -> 1.19 us
where the time goes in v2:
time: 64.7 us; the launch traced here: 64.6 us
  Pallas kernels  62.8 us (97%)
  local copies, waits for them, and re-layouts  1.19 us (2%)
    pallas_call x1, Pallas kernels, per_device(): pl.pallas_call(functools.partial(kernel, nl, ns, ny), out_shape=(jax.Shap...  62.8 us

profile of v2, /device:TPU:1, one launch (start us, length us, event | category | flops | bytes accessed | tf_op | source)
XLA Modules:
  0.0 64.6 jit_solution(9637724583969776952)
XLA Ops:
  0.6 62.8 %shard_map.113 = (f32[4,4,256]{2,1,0:T(4,128)S(1)}, f32[4,3]{1,0:T(4,128)S(1)}) custom-call(s32[1,4]{1,0:T(1,128)} %bitcast.3, s32[2,4]{1,0:T(2,128)} %bitcast.2, s32[1,4]{1,0:T(1,128)} %top_ids_h.1, f32[4,256]{1,0:T(4,128)} %start_h.1, bf16[4,2,256,256]{3,2,1,0:T(8,128)(2,1)} %near_h.1, bf16[4,64,256]{2,1,0:T(8,128)(2,1)} %lb_h.1, ...), custom_call_target="tpu_custom_call" | custom-call | tf_op jit(solution)/shard_map/pallas_call | solution.py:488
  63.4 0.6 copy.14
  64.0 0.6 copy.15

commit v3 on v2

--- a/solution.py
+++ b/solution.py
@@ -105,8 +105,6 @@
         (top_ids_h, top_ids),
     )
     loads = [pltpu.make_async_copy(s, d, in_sem.at[i]) for i, (s, d) in enumerate(pairs)]
-    for load in loads:
-        load.start()
 
     columns = [lax.rem(y + outward(j, ny), ny) for j in range(ny)]
 
@@ -139,6 +137,8 @@
 
     each_branch(greet_branch)
     lax.fori_loop(1, 3 * ns, greet_halo, 0)
+    for load in loads:
+        load.start()
 
     row4 = lax.broadcasted_iota(jnp.int32, (4, 256), 0)
     row8 = lax.broadcasted_iota(jnp.int32, (8, 256), 0)
@@ -221,7 +221,7 @@
 
     def send_x(k):
         def go(j, c):
-            to, other, slot = halo_at(j)
+            to, other, slot = halo_at(3 * ns - j)
             pltpu.make_async_remote_copy(
                 xall[k].at[ns + sub],
                 xall[k].at[slot * ns + sub],
@@ -381,18 +381,21 @@
         else:
             alpha = jnp.full((1, 1), 2.0**-20, F32)
         nus.append(1.0 / alpha)
-        scaled = branchl * (alpha * (1.0 / total))
-        factors = jnp.where(low, alpha * (2.0 * sums[0] + added), branchc[0])
-        first = sums[1] * jnp.where(low, alpha * alpha, alpha) + scaled * factors
-        pending = put(pending, k + 1, k + 1, half_sum(first, 0))
-        pending = put(pending, k + 1, 0, half_sum(first, 1))
-        if k >= 1:
-            second = sums[2] * alpha + scaled * jnp.where(low, branchc[1], branchc[k])
-            pending = put(pending, k + 1, 1, half_sum(second, 0))
-            if k == 2:
-                pending = put(pending, 3, 2, half_sum(second, 1))
+        def inner_products(row):
+            scaled = branchl * (alpha * (1.0 / total))
+            factors = jnp.where(low, alpha * (2.0 * sums[0] + added), branchc[0])
+            first = sums[1] * jnp.where(low, alpha * alpha, alpha) + scaled * factors
+            row = put(row, k + 1, k + 1, half_sum(first, 0))
+            row = put(row, k + 1, 0, half_sum(first, 1))
+            if k >= 1:
+                second = sums[2] * alpha + scaled * jnp.where(low, branchc[1], branchc[k])
+                row = put(row, k + 1, 1, half_sum(second, 0))
+                if k == 2:
+                    row = put(row, 3, 2, half_sum(second, 1))
+            return row
+
         if k == 2:
-            r2[3][leaf] = pending
+            r2[3][leaf] = inner_products(pending)
             send_r2(3)
         down = jnp.sum(dot_nn(split(branchl[:, :64]), t_v[...]), axis=0, keepdims=True)
         down = jnp.concatenate([down[:, 256 * i : 256 * (i + 1)] for i in range(4)], axis=0)
@@ -401,9 +404,10 @@
         if k < 2:
             x8 = split(x)
             exchange_leaves(k + 1, x, x8)
+            own = own_part(x8)
+            pending = inner_products(pending)
             branchc.append(later * alpha)
             before = alpha
-            own = own_part(x8)
 
     bytes_wait(r2[3].at[pl.ds(0, nl - 1)], r2_recv.at[3])
     sums = over_table(3, "sum")

time: 64.7 us -> 64.7 us (level)
  no operation moved by 1% of the time
where the time goes in v3:
time: 64.7 us; the launch traced here: 64.6 us
  Pallas kernels  62.8 us (97%)
  local copies, waits for them, and re-layouts  1.19 us (2%)
    pallas_call x1, Pallas kernels, per_device(): pl.pallas_call(functools.partial(kernel, nl, ns, ny), out_shape=(jax.Shap...  62.8 us

profile of v3, /device:TPU:1, one launch (start us, length us, event | category | flops | bytes accessed | tf_op | source)
XLA Modules:
  0.0 64.6 jit_solution(16082401267071013457)
XLA Ops:
  0.6 62.8 %shard_map.113 = (f32[4,4,256]{2,1,0:T(4,128)S(1)}, f32[4,3]{1,0:T(4,128)S(1)}) custom-call(s32[1,4]{1,0:T(1,128)} %bitcast.3, s32[2,4]{1,0:T(2,128)} %bitcast.2, s32[1,4]{1,0:T(1,128)} %top_ids_h.1, f32[4,256]{1,0:T(4,128)} %start_h.1, bf16[4,2,256,256]{3,2,1,0:T(8,128)(2,1)} %near_h.1, bf16[4,64,256]{2,1,0:T(8,128)(2,1)} %lb_h.1, ...), custom_call_target="tpu_custom_call" | custom-call | tf_op jit(solution)/shard_map/pallas_call | solution.py:492
  63.4 0.6 copy.14
  64.0 0.6 copy.15

commit v4 on v2

--- a/solution.py
+++ b/solution.py
@@ -265,7 +265,6 @@
 
     def partner_part(k):
         bytes_wait(xall[k].at[pl.ds(0, 3 * ns - 1)], x_recv.at[k])
-        bytes_wait(call[k].at[pl.ds(0, ns - 1)], c_recv.at[k])
         near_rows, far_rows = [], []
         for i in range(4):
             one = near_ids[0, i]
@@ -275,6 +274,13 @@
             )
             keep = jnp.where(outside, 0.0, 1.0)
             near_rows.append(xall[k][one // 4, one % 4] * keep)
+        p8 = split(jnp.concatenate(near_rows, axis=0))
+        out = jnp.zeros((4, 256), F32)
+        for i in range(4):
+            o8 = dot_nt(p8, near_v[i, 1])
+            out = jnp.where(row4 == i, o8[:4] + o8[4:], out)
+        bytes_wait(call[k].at[pl.ds(0, ns - 1)], c_recv.at[k])
+        for i in range(4):
             first, second = far_ids[0, i], far_ids[1, i]
             far_rows.append(
                 jnp.where(
@@ -283,14 +289,11 @@
                     call[k][second // 4, second % 4],
                 )
             )
-        p8 = split(jnp.concatenate(near_rows, axis=0))
         f8 = split(jnp.concatenate(far_rows, axis=0))
-        out = jnp.zeros((4, 256), F32)
-        for i in range(4):
-            o8 = dot_nt(p8, near_v[i, 1])
+        for i in range(4):
             g8 = dot_nt(f8, lc_v[i])
-            o4 = o8[:4] + o8[4:] + dot_nn((g8[:4] + g8[4:]).astype(BF16), lb_v[i])
-            out = jnp.where(row4 == i, o4, out)
+            o4 = dot_nn((g8[:4] + g8[4:]).astype(BF16), lb_v[i])
+            out = jnp.where(row4 == i, out + o4, out)
         return out
 
     def over_table(k, op):

time: 64.7 us -> 65 us (level)
  no operation moved by 1% of the time
where the time goes in v4:
time: 65 us; the launch traced here: 64.9 us
  Pallas kernels  63.1 us (97%)
  local copies, waits for them, and re-layouts  1.19 us (2%)
    pallas_call x1, Pallas kernels, per_device(): pl.pallas_call(functools.partial(kernel, nl, ns, ny), out_shape=(jax.Shap...  63.1 us

profile of v4, /device:TPU:1, one launch (start us, length us, event | category | flops | bytes accessed | tf_op | source)
XLA Modules:
  0.0 64.9 jit_solution(9831476648151429647)
XLA Ops:
  0.6 63.1 %shard_map.113 = (f32[4,4,256]{2,1,0:T(4,128)S(1)}, f32[4,3]{1,0:T(4,128)S(1)}) custom-call(s32[1,4]{1,0:T(1,128)} %bitcast.3, s32[2,4]{1,0:T(2,128)} %bitcast.2, s32[1,4]{1,0:T(1,128)} %top_ids_h.1, f32[4,256]{1,0:T(4,128)} %start_h.1, bf16[4,2,256,256]{3,2,1,0:T(8,128)(2,1)} %near_h.1, bf16[4,64,256]{2,1,0:T(8,128)(2,1)} %lb_h.1, ...), custom_call_target="tpu_custom_call" | custom-call | tf_op jit(solution)/shard_map/pallas_call | solution.py:491
  63.7 0.6 copy.14
  64.3 0.6 copy.15
